TPU v7x, 32 devices: a whole 2x2x4 slice. The times are simulated.
32 devices in a mesh: rcv: 8 (over z, y), src: 4 (over x, core).
Axes of the slice: x: 2, y: 2, z: 4, core: 2. Of those that a mesh axis runs over, the one named last changes fastest.
Arguments:
- k_op: bfloat16 [2, 3072, 3072], P(None, 'rcv', 'src'), may hold values from -0.078125 to 0.078125
- data: bfloat16 [2, 3072, 3072], P(None, 'rcv', 'src'), may hold values from -6 to 6
- factor: bfloat16 [2, 4, 768, 128], P(None, 'src', 'rcv'), may hold values from -1.796875 to 1.796875
Outputs:
- gradient: float32 [2, 4, 768, 128], P(None, 'src', 'rcv')
All inputs are finite; a program needn't handle non-finite values.
Results may differ from a plain program's by a relative error of at most 0.0019.
Values may be sent and summed in bfloat16 or wider, within the bound.
A program may use at most 64 MiB of HBM per device.

v0:
```python
import math
import jax
import jax.numpy as jnp
from jax import lax
from jax.sharding import PartitionSpec as P


def plain_dot(left, right):
    return jnp.dot(left, right, preferred_element_type=jnp.float32)


def contract_last(left, right):
    return lax.dot_general(
        left, right, (((1,), (1,)), ((), ())), preferred_element_type=jnp.float32
    )


def contract_first(left, right):
    return lax.dot_general(
        left, right, (((0,), (0,)), ((), ())), preferred_element_type=jnp.float32
    )


def body(k_op, data, factor):
    row_count = k_op.shape[1]
    receivers = row_count * lax.axis_size("rcv")
    gathered = lax.all_gather(factor, "rcv", axis=2, tiled=True)
    factor_real = gathered[0, 0]
    factor_imaginary = gathered[1, 0]
    kernel_real = k_op[0]
    kernel_imaginary = k_op[1]
    modeled_part = jnp.stack(
        [
            plain_dot(kernel_real, factor_real) - plain_dot(kernel_imaginary, factor_imaginary),
            plain_dot(kernel_real, factor_imaginary) + plain_dot(kernel_imaginary, factor_real),
        ]
    )
    modeled = lax.psum(modeled_part, "src").astype(jnp.bfloat16)
    modeled_real = modeled[0]
    modeled_imaginary = modeled[1]
    error_real = (
        contract_last(modeled_real, factor_real)
        - contract_last(modeled_imaginary, factor_imaginary)
        - data[0].astype(jnp.float32)
    ).astype(jnp.bfloat16)
    error_imaginary = (
        contract_last(modeled_real, factor_imaginary)
        + contract_last(modeled_imaginary, factor_real)
        - data[1].astype(jnp.float32)
    ).astype(jnp.bfloat16)
    weighted_part = jnp.stack(
        [
            plain_dot(error_real, factor_real) + plain_dot(error_imaginary, factor_imaginary),
            plain_dot(error_imaginary, factor_real) - plain_dot(error_real, factor_imaginary),
        ]
    )
    mirror = jnp.stack(
        [
            contract_first(error_real, modeled_real)
            + contract_first(error_imaginary, modeled_imaginary),
            contract_first(error_imaginary, modeled_real)
            - contract_first(error_real, modeled_imaginary),
        ]
    )
    weighted = lax.psum(weighted_part, "src").astype(jnp.bfloat16)
    weighted_real = weighted[0]
    weighted_imaginary = weighted[1]
    projected = jnp.stack(
        [
            contract_first(kernel_real, weighted_real)
            + contract_first(kernel_imaginary, weighted_imaginary),
            contract_first(kernel_real, weighted_imaginary)
            - contract_first(kernel_imaginary, weighted_real),
        ]
    )
    summed = lax.psum_scatter(projected + mirror, "rcv", scatter_dimension=1, tiled=True)
    scaling = 1.0 / math.sqrt(receivers)
    return (summed * scaling)[:, None]


def solution(mesh):
    return jax.shard_map(
        body,
        mesh=mesh,
        in_specs=(P(None, "rcv", "src"), P(None, "rcv", "src"), P(None, "src", "rcv", None)),
        out_specs=P(None, "src", "rcv", None),
        check_vma=False,
    )
```

profile of v0, /device:TPU:0, one launch (start us, length us, event | category | flops | bytes accessed | tf_op | source)
XLA Modules:
  0.0 163.0 jit_solution(13344070304495948577)
XLA Ops:
  6.5 33.1 %all_gather.3 = bf16[2,1,768,128]{3,2,1,0:T(8,128)(2,1)S(1)} all-gather(bf16[2,1,96,128]{3,2,1,0:T(8,128)(2,1)} %param.5), channel_id=1, replica_groups=mesh['rcv'=8,'src'=4] {'rcv'}, dimensions={2}, use_global_device_ids=true | all-gather | bytes 442368 | tf_op jit(solution)/shard_map/all_gather | solution.py:27
  39.6 1.4 fusion.20
  41.0 0.3 fusion.22
  41.4 0.3 fusion.10
  41.7 0.3 fusion.11
  42.0 14.5 %all-reduce.6 = bf16[2,384,128]{2,1,0:T(8,128)(2,1)S(1)} all-reduce(f32[2,384,128]{2,1,0:T(8,128)S(1)} %pad_maximum_fusion), channel_id=1, replica_groups=mesh['rcv'=8,'src'=4] {'src'}, use_global_device_ids=true, to_apply=%region_0.0 | all-reduce | flops 98304 | bytes 589824 | tf_op jit(solution)/shard_map/psum | solution.py:38
  56.6 0.3 fusion.36
  56.9 0.3 fusion.35
  57.2 0.6 copy-done.1
  58.2 0.3 fusion.33
  58.5 0.3 fusion.2
  58.8 0.3 fusion.34
  59.1 0.3 fusion.8
  59.5 0.3 fusion.9
  59.8 14.4 %all-reduce.7 = bf16[2,384,128]{2,1,0:T(8,128)(2,1)S(1)} all-reduce(f32[2,384,128]{2,1,0:T(8,128)S(1)} %pad_maximum_fusion.1), channel_id=1, replica_groups=mesh['rcv'=8,'src'=4] {'src'}, use_global_device_ids=true, to_apply=%region_1.0 | all-reduce | flops 98304 | bytes 589824 | tf_op jit(solution)/shard_map/psum | solution.py:65
  74.8 0.3 fusion.37
  75.2 0.3 fusion.38
  76.1 0.3 fusion.4
  76.4 0.3 fusion.5
  76.8 1.2 copy.13
  78.0 0.6 dynamic-slice
  79.3 75.3 %all-reduce.5.cloned.1.call-done = f32[2,768,128]{2,0,1:T(2,128)} async-done(((f32[2,768,128]{2,0,1:T(2,128)}), f32[2,768,128]{2,0,1:T(2,128)}) %all-reduce.5.cloned.1.call-update) | async-done | bytes 786448
  154.5 0.9 fusion.32
  155.5 0.6 copy.14
  (15 shorter events, 1.6 us)
Async XLA Ops:
  6.5 34.5 %copy-start = (bf16[2,384,768]{2,1,0:T(8,128)(2,1)S(1)}, bf16[2,384,768]{2,1,0:T(8,128)(2,1)}, u32[]{:S(2)}) copy-start(bf16[2,384,768]{2,1,0:T(8,128)(2,1)} %param.3) | copy-start | bytes 3538948
  6.5 148.0 %all-reduce.5.cloned.1.call-start = ((), (), s32[]{:S(2)}) async-start(), calls=%async_computation | async-start | bytes 1572864
  56.6 1.3 copy-start.1
  76.8 1.2 copy-start.2
Sparse Core Ops, SparseCore 0:
  78.1 76.3 all-reduce.4
where the time goes:
time: 163 us
  waiting for transfers between devices  75.3 us (46%)
  blocking collectives  62.1 us (38%)
  between operations  14.2 us (9%)
  matrix products  7.23 us (4%)
  local copies, waits for them, and re-layouts  3.06 us (2%)
    unnamed x2, waiting for transfers between devices  75.3 us
    all_gather x1, blocking collectives, body(): gathered = lax.all_gather(factor, 'rcv', axis=2, tiled=True)  33.1 us
    psum x1, blocking collectives, body(): modeled = lax.psum(modeled_part, 'src').astype(jnp.bfloat16)  14.5 us
    psum x1, blocking collectives, body(): weighted = lax.psum(weighted_part, 'src').astype(jnp.bfloat16)  14.4 us
    dot_general x8, matrix products, plain_dot(): return jnp.dot(left, right, preferred_element_type=jnp.float32)  3.58 us
  transfers between devices with their start and end apart: 1, of which 1 were waited for; matrix products, arithmetic and copies ran while one was open for 0% of the time, Pallas kernels for 0%

commit v1 on v0

--- a/solution.py
+++ b/solution.py
@@ -35,7 +35,12 @@
             plain_dot(kernel_real, factor_imaginary) + plain_dot(kernel_imaginary, factor_real),
         ]
     )
-    modeled = lax.psum(modeled_part, "src").astype(jnp.bfloat16)
+
+    def render_set(payload):
+        oldest = jnp.sum(lax.all_gather(payload, axis_name="src"), axis=0)
+        return oldest
+
+    modeled = render_set(modeled_part).astype(jnp.bfloat16)
     modeled_real = modeled[0]
     modeled_imaginary = modeled[1]
     error_real = (

time: 163 us -> 172 us (1.055)
  waiting for transfers between devices: 75.3 us -> 95.6 us
  blocking collectives: 62.1 us -> 48 us
  other arithmetic: 1.09 us -> 3.33 us
    all_gather x0 -> x1, waiting for transfers between devices: none -> 20.8 us  [render_set(): oldest = jnp.sum(lax.all_gather(payload, axis_name='src'), axis=0)]
    psum x1 -> x0, blocking collectives: 14.5 us -> none  [body(): modeled = lax.psum(modeled_part, 'src').astype(jnp.bfloat16)]
    unnamed x2 -> x3, waiting for transfers between devices: 75.3 us -> 74.8 us
  transfers between devices with their start and end apart: 1 -> 2, of which waited for: 1 -> 2; matrix products, arithmetic and copies ran while one was open for 0% -> 0% of each run, Pallas kernels for 0% -> 0%
where the time goes in v1:
time: 172 us
  waiting for transfers between devices  95.6 us (56%)
  blocking collectives  48 us (28%)
  between operations  14.2 us (8%)
  matrix products  7.23 us (4%)
  other arithmetic  3.33 us (2%)
  local copies, waits for them, and re-layouts  3.07 us (2%)
    unnamed x3, waiting for transfers between devices  74.8 us
    all_gather x1, blocking collectives, body(): gathered = lax.all_gather(factor, 'rcv', axis=2, tiled=True)  33.1 us
    all_gather x1, waiting for transfers between devices, render_set(): oldest = jnp.sum(lax.all_gather(payload, axis_name='src'), axis=0)  20.8 us
    psum x1, blocking collectives, body(): weighted = lax.psum(weighted_part, 'src').astype(jnp.bfloat16)  14.9 us
    dot_general x8, matrix products, plain_dot(): return jnp.dot(left, right, preferred_element_type=jnp.float32)  3.6 us
  transfers between devices with their start and end apart: 2, of which 2 were waited for; matrix products, arithmetic and copies ran while one was open for 0% of the time, Pallas kernels for 0%

profile of v1, /device:TPU:0, one launch (start us, length us, event | category | flops | bytes accessed | tf_op | source)
XLA Modules:
  0.0 171.5 jit_solution(4635274211374891299)
XLA Ops:
  6.5 33.1 %all_gather.9 = bf16[2,1,768,128]{3,2,1,0:T(8,128)(2,1)S(1)} all-gather(bf16[2,1,96,128]{3,2,1,0:T(8,128)(2,1)} %param.5), channel_id=1, replica_groups=mesh['rcv'=8,'src'=4] {'rcv'}, dimensions={2}, use_global_device_ids=true | all-gather | bytes 442368 | tf_op jit(solution)/shard_map/all_gather | solution.py:27
  39.6 1.4 fusion.20
  41.0 0.3 fusion.22
  41.4 0.3 fusion.10
  41.7 0.3 fusion.11
  42.0 0.8 pad_maximum_fusion
  42.8 20.8 %all-gather.3.cloned.1.call-done = f32[8,384,128]{2,1,0:T(8,128)} async-done(((f32[2,384,128]{2,1,0:T(8,128)}), f32[8,384,128]{2,1,0:T(8,128)}) %all-gather.3.cloned.1.call-update) | async-done | bytes 1572880 | tf_op jit(solution)/shard_map/all_gather | solution.py:40
  63.6 1.5 reduce_sum.9
  65.8 0.6 copy-done.1
  66.4 0.3 fusion.3
  66.8 0.3 fusion.33
  67.1 0.3 fusion.2
  67.4 0.3 fusion.34
  67.7 0.3 fusion.8
  68.0 0.3 fusion.9
  68.4 14.9 %all-reduce.5 = bf16[2,384,128]{2,1,0:T(8,128)(2,1)S(1)} all-reduce(f32[2,384,128]{2,1,0:T(8,128)S(1)} %pad_maximum_fusion.1), channel_id=1, replica_groups=mesh['rcv'=8,'src'=4] {'src'}, use_global_device_ids=true, to_apply=%region_1.0 | all-reduce | flops 98304 | bytes 589824 | tf_op jit(solution)/shard_map/psum | solution.py:70
  83.9 0.3 fusion.37
  85.1 0.3 fusion.4
  85.5 0.3 fusion.5
  85.9 1.2 copy.13
  87.1 0.6 dynamic-slice
  88.3 74.8 %all-reduce.4.cloned.1.call-done = f32[2,768,128]{2,0,1:T(2,128)} async-done(((f32[2,768,128]{2,0,1:T(2,128)}), f32[2,768,128]{2,0,1:T(2,128)}) %all-reduce.4.cloned.1.call-update) | async-done | bytes 786448
  163.1 0.9 fusion.32
  164.0 0.6 copy.14
  (18 shorter events, 2.3 us)
Async XLA Ops:
  6.5 34.5 %copy-start = (bf16[2,384,768]{2,1,0:T(8,128)(2,1)S(1)}, bf16[2,384,768]{2,1,0:T(8,128)(2,1)}, u32[]{:S(2)}) copy-start(bf16[2,384,768]{2,1,0:T(8,128)(2,1)} %param.3) | copy-start | bytes 3538948
  6.5 57.1 %all-gather.3.cloned.1.call-start = ((), (), s32[]{:S(2)}) async-start(), calls=%async_computation | async-start | bytes 1966080 | tf_op jit(solution)/shard_map/all_gather | solution.py:40
  42.8 120.3 %all-reduce.4.cloned.1.call-start = ((), (), s32[]{:S(2)}) async-start(), calls=%async_computation.1 | async-start | bytes 1572864
  65.2 1.3 copy-start.1
  85.9 1.2 copy-start.2
Sparse Core Ops, SparseCore 0:
  42.9 20.6 all-gather.2
  87.2 75.8 all-reduce.3
